TPU v7x, 32 devices: a whole 2x2x4 slice. The times are simulated.
32 devices in a mesh: ctx: 8 (over y, x, core), chan: 4 (over z).
Axes of the slice: x: 2, y: 2, z: 4, core: 2. Of those that a mesh axis runs over, the one named last changes fastest.
Arguments:
- value_branch: bfloat16 [192, 65536], P(None, ('ctx', 'chan')), may hold values from -6 to 6
- key_branch: bfloat16 [192, 65536], P(None, ('ctx', 'chan')), may hold values from -6 to 6
- gate_branch: bfloat16 [192, 65536], P(None, ('ctx', 'chan')), may hold values from -6 to 6
- skip_gain: float32 [192], replicated, may hold values from -4 to 4
- spectra: float32 [2, 192, 8, 8192], P(None, 'chan', 'ctx'), may hold values from -6 to 6
Outputs:
- gated_output: bfloat16 [192, 65536], P(None, ('ctx', 'chan'))
All inputs are finite; a program needn't handle non-finite values.
Results may differ from a plain program's by a relative error of at most 0.0054.
Values may be sent and summed in bfloat16 or wider, within the bound.
A program may use at most 64 MiB of HBM per device.

v0:
```python
import functools
import math

import jax
import jax.numpy as jnp
import numpy as np
from jax import lax
from jax.experimental import pallas as pl
from jax.experimental.pallas import tpu as pltpu
from jax.sharding import PartitionSpec as P

two_pi = 2.0 * math.pi
first_factor = 128
highest = lax.Precision.HIGHEST


def reversed_bits(numbers, bit_count):
    result = numbers * 0
    for bit_number in range(bit_count):
        result = result + (numbers >> bit_number & 1) * (1 << bit_count - 1 - bit_number)
    return result


def phase_pair(radians):
    return (jnp.cos(radians), jnp.sin(radians))


def block_table(length_of, direction):
    counter = jnp.arange(length_of, dtype=jnp.int32)
    product = counter[:, None] * counter[None, :] % length_of
    cosine, sine = phase_pair(direction * two_pi / length_of * product.astype(jnp.float32))
    upper_rows = jnp.stack([cosine, -sine], axis=1)
    lower_rows = jnp.stack([sine, cosine], axis=1)
    return jnp.stack([upper_rows, lower_rows], axis=0)


def complex_mul(signal, factor):
    factor_real, factor_imag = factor
    return jnp.stack(
        [
            signal[0] * factor_real - signal[1] * factor_imag,
            signal[0] * factor_imag + signal[1] * factor_real,
        ]
    )


def forward_local(signal):
    channel_count, seq_length = (signal.shape[1], signal.shape[2])
    second_factor = seq_length // first_factor
    blocked = signal.reshape(2, channel_count, first_factor, second_factor)
    section_one = jnp.einsum(
        "orca,cxaq->oxrq", block_table(first_factor, -1.0), blocked, precision=highest
    )
    column = jnp.arange(first_factor, dtype=jnp.int32)[:, None]
    within = jnp.arange(second_factor, dtype=jnp.int32)[None, :]
    twiddle = phase_pair(-two_pi / seq_length * (column * within).astype(jnp.float32))
    section_two = complex_mul(section_one, twiddle)
    section_three = jnp.einsum(
        "peoq,oxrq->pxer", block_table(second_factor, -1.0), section_two, precision=highest
    )
    return section_three.reshape(2, channel_count, seq_length)


def inverse_local(signal):
    channel_count, seq_length = (signal.shape[1], signal.shape[2])
    second_factor = seq_length // first_factor
    blocked = signal.reshape(2, channel_count, second_factor, first_factor)
    section_one = jnp.einsum(
        "pqoe,oxer->pxqr", block_table(second_factor, 1.0), blocked, precision=highest
    )
    within = jnp.arange(second_factor, dtype=jnp.int32)[:, None]
    column = jnp.arange(first_factor, dtype=jnp.int32)[None, :]
    twiddle = phase_pair(two_pi / seq_length * (within * column).astype(jnp.float32))
    section_two = complex_mul(section_one, twiddle)
    section_three = jnp.einsum(
        "paor,oxqr->pxaq", block_table(first_factor, 1.0), section_two, precision=highest
    )
    return section_three.reshape(2, channel_count, seq_length)


def blockwise_body(value_branch, key_branch, gate_branch, skip_gain, spectra):
    carried = (key_branch.astype(jnp.float32) * value_branch.astype(jnp.float32)).astype(
        jnp.bfloat16
    )
    series = lax.all_to_all(carried, "chan", split_axis=0, concat_axis=1, tiled=True)
    channel_count, seq_length = series.shape
    ctx_count = lax.axis_size("ctx")
    bit_count = ctx_count.bit_length() - 1
    device = lax.axis_index("ctx")
    total_length = seq_length * ctx_count
    counter = jnp.arange(ctx_count, dtype=jnp.int32)
    target = reversed_bits(counter, bit_count)
    blocks = lax.all_to_all(
        series.reshape(channel_count, 1, seq_length), "ctx", split_axis=2, concat_axis=1, tiled=True
    )
    matrix = jnp.stack(
        phase_pair(
            -two_pi
            / ctx_count
            * (target[:, None] * counter[None, :] % ctx_count).astype(jnp.float32)
        )
    )
    rows = jnp.einsum("ojp,xps->oxjs", matrix, blocks.astype(jnp.float32), precision=highest)
    received = lax.all_to_all(rows, "ctx", split_axis=2, concat_axis=3, tiled=True)
    signal = received.reshape(2, channel_count, seq_length)
    device_rank = reversed_bits(device, bit_count)
    positions = jnp.arange(seq_length, dtype=jnp.int32)
    radians = two_pi / total_length * (positions * device_rank).astype(jnp.float32)
    signal = complex_mul(signal, phase_pair(-radians))
    spectrum = forward_local(signal)
    shaped = complex_mul(spectrum, (spectra[0, :, 0, :], spectra[1, :, 0, :]))
    returned = complex_mul(inverse_local(shaped), phase_pair(radians))
    parts = lax.all_to_all(
        returned.reshape(2, channel_count, 1, seq_length),
        "ctx",
        split_axis=3,
        concat_axis=2,
        tiled=True,
    )
    cosine, sine = phase_pair(
        two_pi / ctx_count * (counter[:, None] * target[None, :] % ctx_count).astype(jnp.float32)
    )
    matrix = jnp.stack([cosine, -sine])
    summed = jnp.einsum("opj,oxjs->xps", matrix, parts, precision=highest) / total_length
    local_conv = summed.astype(jnp.bfloat16)
    convolved = lax.all_to_all(local_conv, "ctx", split_axis=1, concat_axis=2, tiled=True).reshape(
        channel_count, seq_length
    )
    tokens_conv = lax.all_to_all(convolved, "chan", split_axis=1, concat_axis=0, tiled=True)
    result = gate_branch.astype(jnp.float32) * (
        tokens_conv.astype(jnp.float32) + skip_gain[:, None] * carried.astype(jnp.float32)
    )
    return result.astype(jnp.bfloat16)


lanes = 128
MESH = pl.DeviceIdType.MESH
VMEM = pl.BlockSpec(memory_space=pltpu.VMEM)


@functools.lru_cache(maxsize=None)
def transform_tables(rows_total, ctx_count):
    length = rows_total * lanes
    bit_count = ctx_count.bit_length() - 1
    rev = np.array([int(format(j, "b").zfill(bit_count)[::-1], 2) if bit_count else 0 for j in range(ctx_count)])
    a = np.arange(rows_total // ctx_count)
    k1 = (rev[:, None] + ctx_count * a[None, :]).reshape(-1)
    fold = lanes // (rows_total // ctx_count)
    k2 = np.arange(lanes).reshape(lanes // fold, fold).T.reshape(-1)
    n1, n2 = np.arange(rows_total), np.arange(lanes)
    f1 = np.exp(-2j * np.pi * (np.outer(k1, n1) % rows_total) / rows_total)
    f2 = np.exp(-2j * np.pi * (np.outer(n2, k2) % lanes) / lanes)
    tw = np.exp(-2j * np.pi * (np.outer(k1, n2) % length) / length)
    w1 = np.stack([f1.real, f1.imag])
    w2 = np.block([[f2.real, f2.imag], [-f2.imag, f2.real]])
    b2 = f2.conj().T
    w3 = np.block([[b2.real, b2.imag], [-b2.imag, b2.real]])
    b1 = f1.conj().T / length
    v1 = np.concatenate([b1.real, -b1.imag], axis=1)
    half = lambda t: np.asarray(t, dtype=jnp.bfloat16)
    return half(w1), half(w2), half(w3), half(v1), np.stack([tw.real, tw.imag]).astype(np.float32)


def greet_all(ctx_count, chan_count, me):
    total = ctx_count * chan_count
    barrier = pltpu.get_barrier_semaphore()

    @pl.loop(1, total)
    def _(offset):
        other = lax.rem(me + offset, total)
        pl.semaphore_signal(
            barrier, inc=1, device_id=(other // chan_count, lax.rem(other, chan_count)), device_id_type=MESH
        )

    pl.semaphore_wait(barrier, total - 1)


def dot(a, b):
    return jnp.dot(a, b, preferred_element_type=jnp.float32)


def fused_kernel(
    ctx_count, chan_count, c_ref, s_hbm, *refs
):
    tables_hbm, (o_ref,), tables = refs[:5], refs[5:6], refs[6:11]
    w1_ref, w2_ref, w3_ref, v1_ref, tw_ref = tables
    s_ref, stage, r_ref, x_ref, y_ref, g_ref = refs[11:17]
    send_c, recv_c, send_s, recv_s, send_y, recv_y, local = refs[17:]
    ctx, chan = lax.axis_index("ctx"), lax.axis_index("chan")
    me = ctx * chan_count + chan
    total = ctx_count * chan_count
    pairs, rows = x_ref.shape[0], c_ref.shape[1]
    rows_total = x_ref.shape[1]
    block = stage.shape[2]
    local_channels = stage.shape[1]

    loads = [pltpu.make_async_copy(s_hbm, s_ref, local.at[0])]
    for i, (source, target) in enumerate(zip(tables_hbm, tables)):
        loads.append(pltpu.make_async_copy(source, target, local.at[1 + i]))
    for load in loads:
        load.start()
    greet_all(ctx_count, chan_count, me)

    def place(offset):
        other = lax.rem(me + offset, total)
        return other, other // chan_count, lax.rem(other, chan_count)

    def slot(ctx_index, chan_index):
        return (chan_index * ctx_count + ctx_index) * pairs

    my_rows = pl.ds(pl.multiple_of(me * rows, rows), rows)
    my_block = pl.ds(pl.multiple_of(ctx * block, block), block)

    def carried_copy(pair, offset):
        other, other_ctx, other_chan = place(offset)
        return pltpu.make_async_remote_copy(
            src_ref=c_ref.at[slot(other_ctx, other_chan) + pair],
            dst_ref=x_ref.at[pair, my_rows],
            send_sem=send_c.at[pair, offset - 1],
            recv_sem=recv_c.at[pair, offset - 1],
            device_id=(other_ctx, other_chan),
            device_id_type=MESH,
        )

    def spectra_copy(pair, offset):
        other_ctx = lax.rem(ctx + offset, ctx_count)
        return pltpu.make_async_remote_copy(
            src_ref=stage.at[:, pl.ds((other_ctx * pairs + pair) * 2, 2)],
            dst_ref=r_ref.at[:, pl.ds(2 * pair, 2), my_block],
            send_sem=send_s.at[pair, offset - 1],
            recv_sem=recv_s.at[pair, offset - 1],
            device_id=(other_ctx, chan),
            device_id_type=MESH,
        )

    def result_copy(pair, offset):
        other, other_ctx, other_chan = place(offset)
        return pltpu.make_async_remote_copy(
            src_ref=y_ref.at[pair, pl.ds(pl.multiple_of(other * rows, rows), rows)],
            dst_ref=o_ref.at[slot(ctx, chan) + pair],
            send_sem=send_y.at[pair, offset - 1],
            recv_sem=recv_y.at[pair, offset - 1],
            device_id=(other_ctx, other_chan),
            device_id_type=MESH,
        )

    def each(copy_of, pair, count, act):
        @pl.loop(1, count)
        def _(offset):
            act(copy_of(pair, offset))

    def turned(part, channel):
        flipped = s_ref[part * local_channels + channel].T
        pieces = [flipped[f * block : (f + 1) * block] for f in range(flipped.shape[0] // block)]
        return jnp.concatenate(pieces, axis=1).astype(jnp.bfloat16)

    start = lambda copy: copy.start()
    for pair in range(pairs):
        each(carried_copy, pair, total, start)
        if pair == 0:
            loads[0].wait()

        @pl.loop(1, ctx_count)
        def _(offset):
            first = (lax.rem(ctx + offset, ctx_count) * pairs + pair) * 2
            for part in range(2):
                for which in range(2):
                    stage[part, first + which] = turned(part, first + which)

        for part in range(2):
            for which in range(2):
                r_ref[part, 2 * pair + which, my_block] = turned(part, (ctx * pairs + pair) * 2 + which)
        x_ref[pair, my_rows] = c_ref[slot(ctx, chan) + pair]
        each(spectra_copy, pair, ctx_count, start)

    for load in loads[1:]:
        load.wait()
    chunk = 128
    for pair in range(pairs):
        each(carried_copy, pair, total, lambda copy: copy.wait_recv())
        each(spectra_copy, pair, ctx_count, lambda copy: copy.wait_recv())
        x = x_ref.at[pair]

        @pl.loop(0, rows_total // chunk)
        def _(step):
            at = pl.ds(pl.multiple_of(step * chunk, chunk), chunk)
            below = pl.ds(pl.multiple_of(rows_total + step * chunk, chunk), chunk)
            real, imag = dot(w1_ref[0, at], x[...]), dot(w1_ref[1, at], x[...])
            t_real, t_imag = tw_ref[0, at], tw_ref[1, at]
            for which in range(2):
                cols = slice(which * lanes, (which + 1) * lanes)
                a_real, a_imag = real[:, cols], imag[:, cols]
                twiddled = jnp.concatenate(
                    [a_real * t_real - a_imag * t_imag, a_real * t_imag + a_imag * t_real], axis=1
                )
                bins = dot(twiddled.astype(jnp.bfloat16), w2_ref[...])
                b_real, b_imag = bins[:, :lanes], bins[:, lanes:]
                f_real = r_ref[0, 2 * pair + which, at].astype(jnp.float32)
                f_imag = r_ref[1, 2 * pair + which, at].astype(jnp.float32)
                shaped = jnp.concatenate(
                    [b_real * f_real - b_imag * f_imag, b_real * f_imag + b_imag * f_real], axis=1
                )
                back = dot(shaped.astype(jnp.bfloat16), w3_ref[...])
                z_real, z_imag = back[:, :lanes], back[:, lanes:]
                g_ref[at, cols] = (z_real * t_real + z_imag * t_imag).astype(jnp.bfloat16)
                g_ref[below, cols] = (z_imag * t_real - z_real * t_imag).astype(jnp.bfloat16)

        @pl.loop(0, rows_total // chunk)
        def _(step):
            at = pl.ds(pl.multiple_of(step * chunk, chunk), chunk)
            y_ref[pair, at] = dot(v1_ref[at], g_ref[...]).astype(jnp.bfloat16)

        o_ref[slot(ctx, chan) + pair] = y_ref[pair, my_rows]
        each(result_copy, pair, total, start)

    for pair in range(pairs):
        each(carried_copy, pair, total, lambda copy: copy.wait_send())
        each(spectra_copy, pair, ctx_count, lambda copy: copy.wait_send())
        each(result_copy, pair, total, lambda copy: copy.wait())


def channel_body(value_branch, key_branch, gate_branch, skip_gain, spectra):
    channels, tokens = value_branch.shape
    ctx_count, chan_count = lax.axis_size("ctx"), lax.axis_size("chan")
    total = ctx_count * chan_count
    rows = tokens // lanes
    rows_total = rows * total
    pairs = channels // total // 2
    carried = (key_branch.astype(jnp.float32) * value_branch.astype(jnp.float32)).astype(jnp.bfloat16)
    paired = carried.reshape(channels // 2, 2, rows, lanes).swapaxes(1, 2).reshape(channels // 2, rows, 2 * lanes)
    local_channels = spectra.shape[1]
    block = spectra.shape[3] // lanes
    tables = [jnp.asarray(t) for t in transform_tables(rows_total, ctx_count)]
    sems = lambda *shape: pltpu.SemaphoreType.DMA(shape)
    hbm = pl.BlockSpec(memory_space=pl.ANY)
    gathered = pl.pallas_call(
        functools.partial(fused_kernel, ctx_count, chan_count),
        in_specs=[VMEM] + [hbm] * 6,
        out_specs=VMEM,
        out_shape=jax.ShapeDtypeStruct((channels // 2, rows, 2 * lanes), jnp.bfloat16),
        scratch_shapes=[pltpu.VMEM(t.shape, t.dtype) for t in tables]
        + [
            pltpu.VMEM((2 * local_channels, block, lanes), jnp.float32),
            pltpu.VMEM((2, local_channels, block, lanes), jnp.bfloat16),
            pltpu.VMEM((2, 2 * pairs, rows_total, lanes), jnp.bfloat16),
            pltpu.VMEM((pairs, rows_total, 2 * lanes), jnp.bfloat16),
            pltpu.VMEM((pairs, rows_total, 2 * lanes), jnp.bfloat16),
            pltpu.VMEM((2 * rows_total, 2 * lanes), jnp.bfloat16),
        ]
        + [sems(pairs, count - 1) for count in (total, total, ctx_count, ctx_count, total, total)]
        + [sems(6)],
        compiler_params=pltpu.CompilerParams(collective_id=0, has_side_effects=True),
    )(paired, spectra.reshape(2 * local_channels, block, lanes), *tables)
    tokens_conv = gathered.reshape(channels // 2, rows, 2, lanes).swapaxes(1, 2).reshape(channels, tokens)
    result = gate_branch.astype(jnp.float32) * (
        tokens_conv.astype(jnp.float32) + skip_gain[:, None] * carried.astype(jnp.float32)
    )
    return result.astype(jnp.bfloat16)


def body(value_branch, key_branch, gate_branch, skip_gain, spectra):
    channels, tokens = value_branch.shape
    ctx_count, chan_count = lax.axis_size("ctx"), lax.axis_size("chan")
    total = ctx_count * chan_count
    block_rows = tokens * chan_count // lanes
    fits = (
        channels % (2 * total) == 0
        and tokens % (16 * lanes) == 0
        and block_rows <= lanes
        and lanes % block_rows == 0
        and (tokens * total // lanes) % lanes == 0
    )
    chosen = channel_body if fits else blockwise_body
    return chosen(value_branch, key_branch, gate_branch, skip_gain, spectra)


def solution(mesh):
    in_specs = (
        P(None, ("ctx", "chan")),
        P(None, ("ctx", "chan")),
        P(None, ("ctx", "chan")),
        P(),
        P(None, "chan", "ctx", None),
    )
    out_specs = P(None, ("ctx", "chan"))
    return jax.shard_map(body, mesh=mesh, in_specs=in_specs, out_specs=out_specs, check_vma=False)
```

profile of v0, /device:TPU:0, one launch (start us, length us, event | category | flops | bytes accessed | tf_op | source)
XLA Modules:
  0.0 62.8 jit_solution(11646770128384678754)
XLA Ops:
  0.0 1.6 %fusion.2 = bf16[24,8,16,128]{3,1,2,0:T(8,128)(2,1)S(1)} fusion(bf16[192,2048]{1,0:T(8,128)(2,1)} %param.10, bf16[192,2048]{1,0:T(8,128)(2,1)} %param.11), kind=kLoop, calls=%fused_computation.5 | loop fusion | flops 1572864 | bytes 2359296
  1.6 0.2 copy.13
  1.8 0.6 copy.17
  2.4 1.4 %reshape.17.c_ref = bf16[96,16,256]{2,1,0:T(8,128)(2,1)} reshape(bf16[96,16,2,128]{3,2,1,0:T(2,128)(2,1)S(1)} %bitcast.20) | data formatting | bytes 1572864 | tf_op jit(solution)/shard_map/reshape | solution.py:330
  3.8 53.4 %shard_map.100 = bf16[96,16,256]{2,1,0:T(8,128)(2,1)} custom-call(bf16[96,16,256]{2,1,0:T(8,128)(2,1)} %reshape.17.c_ref, f32[96,64,128]{2,1,0:T(8,128)} %bitcast.21, bf16[2,512,512]{2,1,0:T(8,128)(2,1)} %constant.10.clone.refs_0_, bf16[256,256]{1,0:T(8,128)(2,1)} %constant.11.clone.refs_1_, bf16[256,256]{1,0:T(8,128)(2,1)} %constant.12.clone.refs_2_, ...), custom_call_target="tpu_custom_call" | custom-call | tf_op jit(solution)/shard_map/pallas_call | solution.py:336
  57.2 2.0 %reshape.20 = f32[96,16,2,128]{3,2,1,0:T(2,128)S(1)} reshape(bf16[96,16,256]{2,1,0:T(8,128)(2,1)} %shard_map.100) | data formatting | bytes 2359296 | tf_op jit(solution)/shard_map/convert_element_type | solution.py:356
  59.2 0.0 copy-start
  59.2 0.0 copy-start.1
  59.2 0.0 copy-start.2
  59.3 0.0 copy-start.3
  59.3 0.1 copy.12
  59.4 1.0 %copy-done = bf16[192,2048]{1,0:T(8,128)(2,1)S(1)} copy-done((bf16[192,2048]{1,0:T(8,128)(2,1)S(1)}, bf16[192,2048]{1,0:T(8,128)(2,1)}, u32[]{:S(2)}) %copy-start) | copy-done | bytes 786456
  60.4 0.2 copy-done.1
  60.6 0.2 copy-done.2
  60.8 0.0 copy-done.3
  60.8 1.9 %fusion.1 = bf16[192,2048]{1,0:T(8,128)(2,1)} fusion(f32[24,8,16,128]{3,2,1,0:T(8,128)S(1)} %bitcast.18, bf16[192,2048]{1,0:T(8,128)(2,1)S(1)} %copy-done.2, f32[192]{0:T(256)S(1)} %copy-done.3, bf16[192,2048]{1,0:T(8,128)(2,1)S(1)} %copy-done, bf16[192,2048]{1,0:T(8,128)(2,1)S(1)} %copy-done.1), kind=kLoop, calls=%fused_computation.2 | loop fusion | flops 3932160 | bytes 4719360 | tf_op jit(solution)/shard_map/convert_element_type | solution.py:358
Async XLA Ops:
  59.2 1.1 %copy-start = (bf16[192,2048]{1,0:T(8,128)(2,1)S(1)}, bf16[192,2048]{1,0:T(8,128)(2,1)}, u32[]{:S(2)}) copy-start(bf16[192,2048]{1,0:T(8,128)(2,1)} %param.10) | copy-start | bytes 2359300
  59.2 1.4 %copy-start.1 = (bf16[192,2048]{1,0:T(8,128)(2,1)S(1)}, bf16[192,2048]{1,0:T(8,128)(2,1)}, u32[]{:S(2)}) copy-start(bf16[192,2048]{1,0:T(8,128)(2,1)} %param.11) | copy-start | bytes 2359300
  59.2 1.6 %copy-start.2 = (bf16[192,2048]{1,0:T(8,128)(2,1)S(1)}, bf16[192,2048]{1,0:T(8,128)(2,1)}, u32[]{:S(2)}) copy-start(bf16[192,2048]{1,0:T(8,128)(2,1)} %param.12) | copy-start | bytes 2359300
  59.3 1.6 %copy-start.3 = (f32[192]{0:T(256)S(1)}, f32[192]{0:T(256)}, u32[]{:S(2)}) copy-start(f32[192]{0:T(256)} %param.13) | copy-start | bytes 2308
where the time goes:
time: 63 us; the launch traced here: 62.8 us
  Pallas kernels  53.4 us (85%)
  local copies, waits for them, and re-layouts  5.76 us (9%)
  other arithmetic  3.56 us (6%)
    pallas_call x1, Pallas kernels, channel_body(): pl.pallas_call(functools.partial(fused_kernel, ctx_count, chan_count), in...  53.4 us
    convert_element_type x2, local copies, waits for them, and re-layouts, channel_body(): tokens_conv.astype(jnp.float32)  2.14 us
    reshape x2, local copies, waits for them, and re-layouts, channel_body(): carried.reshape(channels // 2, 2, rows, lanes).swapaxes(1, 2)  2 us
    convert_element_type x1, other arithmetic, channel_body(): return result.astype(jnp.bfloat16)  1.95 us
    unnamed x9, local copies, waits for them, and re-layouts  1.61 us
    unnamed x1, other arithmetic  1.61 us

commit v1 on v0

--- a/solution.py
+++ b/solution.py
@@ -172,20 +172,17 @@
             barrier, inc=1, device_id=(other // chan_count, lax.rem(other, chan_count)), device_id_type=MESH
         )
 
-    pl.semaphore_wait(barrier, total - 1)
-
 
 def dot(a, b):
     return jnp.dot(a, b, preferred_element_type=jnp.float32)
 
 
-def fused_kernel(
-    ctx_count, chan_count, c_ref, s_hbm, *refs
-):
-    tables_hbm, (o_ref,), tables = refs[:5], refs[5:6], refs[6:11]
+def fused_kernel(ctx_count, chan_count, skip_ref, v_hbm, k_hbm, gate_hbm, s_hbm, *refs):
+    tables_hbm, (out_ref,), tables = refs[:5], refs[5:6], refs[6:11]
     w1_ref, w2_ref, w3_ref, v1_ref, tw_ref = tables
     s_ref, stage, r_ref, x_ref, y_ref, g_ref = refs[11:17]
-    send_c, recv_c, send_s, recv_s, send_y, recv_y, local = refs[17:]
+    v_ref, k_ref, gate_ref, c_ref, o_ref = refs[17:22]
+    send_c, recv_c, send_s, recv_s, send_y, recv_y, local = refs[22:]
     ctx, chan = lax.axis_index("ctx"), lax.axis_index("chan")
     me = ctx * chan_count + chan
     total = ctx_count * chan_count
@@ -194,19 +191,34 @@
     block = stage.shape[2]
     local_channels = stage.shape[1]
 
-    loads = [pltpu.make_async_copy(s_hbm, s_ref, local.at[0])]
-    for i, (source, target) in enumerate(zip(tables_hbm, tables)):
-        loads.append(pltpu.make_async_copy(source, target, local.at[1 + i]))
+    greet_all(ctx_count, chan_count, me)
+    sources = (v_hbm, k_hbm, s_hbm, gate_hbm, *tables_hbm)
+    targets = (v_ref, k_ref, s_ref, gate_ref, *tables)
+    loads = [
+        pltpu.make_async_copy(source, target, local.at[i]) for i, (source, target) in enumerate(zip(sources, targets))
+    ]
     for load in loads:
         load.start()
-    greet_all(ctx_count, chan_count, me)
+    group = 2 * ctx_count
+    loads[0].wait()
+    loads[1].wait()
+
+    @pl.loop(0, v_ref.shape[0] // group)
+    def _(index):
+        at = pl.ds(pl.multiple_of(index * group, group), group)
+        product = (k_ref[at].astype(jnp.float32) * v_ref[at].astype(jnp.float32)).astype(jnp.bfloat16)
+        split = product.astype(jnp.float32).reshape(ctx_count, 2, rows, lanes)
+        packed = jnp.concatenate([split[:, 0], split[:, 1]], axis=2)
+        c_ref[pl.ds(index * ctx_count, ctx_count)] = packed.astype(jnp.bfloat16)
+
+    pl.semaphore_wait(pltpu.get_barrier_semaphore(), total - 1)
 
     def place(offset):
         other = lax.rem(me + offset, total)
         return other, other // chan_count, lax.rem(other, chan_count)
 
-    def slot(ctx_index, chan_index):
-        return (chan_index * ctx_count + ctx_index) * pairs
+    def slot(ctx_index, chan_index, pair):
+        return (chan_index * pairs + pair) * ctx_count + ctx_index
 
     my_rows = pl.ds(pl.multiple_of(me * rows, rows), rows)
     my_block = pl.ds(pl.multiple_of(ctx * block, block), block)
@@ -214,7 +226,7 @@
     def carried_copy(pair, offset):
         other, other_ctx, other_chan = place(offset)
         return pltpu.make_async_remote_copy(
-            src_ref=c_ref.at[slot(other_ctx, other_chan) + pair],
+            src_ref=c_ref.at[slot(other_ctx, other_chan, pair)],
             dst_ref=x_ref.at[pair, my_rows],
             send_sem=send_c.at[pair, offset - 1],
             recv_sem=recv_c.at[pair, offset - 1],
@@ -225,7 +237,7 @@
     def spectra_copy(pair, offset):
         other_ctx = lax.rem(ctx + offset, ctx_count)
         return pltpu.make_async_remote_copy(
-            src_ref=stage.at[:, pl.ds((other_ctx * pairs + pair) * 2, 2)],
+            src_ref=stage.at[:, pl.ds((pair * ctx_count + other_ctx) * 2, 2)],
             dst_ref=r_ref.at[:, pl.ds(2 * pair, 2), my_block],
             send_sem=send_s.at[pair, offset - 1],
             recv_sem=recv_s.at[pair, offset - 1],
@@ -237,7 +249,7 @@
         other, other_ctx, other_chan = place(offset)
         return pltpu.make_async_remote_copy(
             src_ref=y_ref.at[pair, pl.ds(pl.multiple_of(other * rows, rows), rows)],
-            dst_ref=o_ref.at[slot(ctx, chan) + pair],
+            dst_ref=o_ref.at[slot(ctx, chan, pair)],
             send_sem=send_y.at[pair, offset - 1],
             recv_sem=recv_y.at[pair, offset - 1],
             device_id=(other_ctx, other_chan),
@@ -258,24 +270,24 @@
     for pair in range(pairs):
         each(carried_copy, pair, total, start)
         if pair == 0:
-            loads[0].wait()
+            loads[2].wait()
 
         @pl.loop(1, ctx_count)
         def _(offset):
-            first = (lax.rem(ctx + offset, ctx_count) * pairs + pair) * 2
+            first = (pair * ctx_count + lax.rem(ctx + offset, ctx_count)) * 2
             for part in range(2):
                 for which in range(2):
                     stage[part, first + which] = turned(part, first + which)
 
         for part in range(2):
             for which in range(2):
-                r_ref[part, 2 * pair + which, my_block] = turned(part, (ctx * pairs + pair) * 2 + which)
-        x_ref[pair, my_rows] = c_ref[slot(ctx, chan) + pair]
+                r_ref[part, 2 * pair + which, my_block] = turned(part, (pair * ctx_count + ctx) * 2 + which)
+        x_ref[pair, my_rows] = c_ref[slot(ctx, chan, pair)]
         each(spectra_copy, pair, ctx_count, start)
 
-    for load in loads[1:]:
+    for load in loads[3:]:
         load.wait()
-    chunk = 128
+    chunk = 2 * lanes
     for pair in range(pairs):
         each(carried_copy, pair, total, lambda copy: copy.wait_recv())
         each(spectra_copy, pair, ctx_count, lambda copy: copy.wait_recv())
@@ -310,13 +322,30 @@
             at = pl.ds(pl.multiple_of(step * chunk, chunk), chunk)
             y_ref[pair, at] = dot(v1_ref[at], g_ref[...]).astype(jnp.bfloat16)
 
-        o_ref[slot(ctx, chan) + pair] = y_ref[pair, my_rows]
+        o_ref[slot(ctx, chan, pair)] = y_ref[pair, my_rows]
         each(result_copy, pair, total, start)
+
+    for pair in range(pairs):
+        each(result_copy, pair, total, lambda copy: copy.wait_recv())
+
+        @pl.loop(0, chan_count)
+        def _(chan_index):
+            first = slot(0, chan_index, pair)
+            sums = []
+            for i in range(ctx_count):
+                for which in range(2):
+                    cols = slice(which * lanes, (which + 1) * lanes)
+                    carried = c_ref[first + i, :, cols].astype(jnp.float32)
+                    gain = skip_ref[2 * (first + i) + which]
+                    sums.append(o_ref[first + i, :, cols].astype(jnp.float32) + gain * carried)
+            flat = jnp.stack(sums).reshape(group, rows * lanes)
+            at = pl.ds(pl.multiple_of(first * 2, group), group)
+            out_ref[at] = (gate_ref[at].astype(jnp.float32) * flat).astype(jnp.bfloat16)
 
     for pair in range(pairs):
         each(carried_copy, pair, total, lambda copy: copy.wait_send())
         each(spectra_copy, pair, ctx_count, lambda copy: copy.wait_send())
-        each(result_copy, pair, total, lambda copy: copy.wait())
+        each(result_copy, pair, total, lambda copy: copy.wait_send())
 
 
 def channel_body(value_branch, key_branch, gate_branch, skip_gain, spectra):
@@ -326,18 +355,18 @@
     rows = tokens // lanes
     rows_total = rows * total
     pairs = channels // total // 2
-    carried = (key_branch.astype(jnp.float32) * value_branch.astype(jnp.float32)).astype(jnp.bfloat16)
-    paired = carried.reshape(channels // 2, 2, rows, lanes).swapaxes(1, 2).reshape(channels // 2, rows, 2 * lanes)
     local_channels = spectra.shape[1]
     block = spectra.shape[3] // lanes
     tables = [jnp.asarray(t) for t in transform_tables(rows_total, ctx_count)]
     sems = lambda *shape: pltpu.SemaphoreType.DMA(shape)
     hbm = pl.BlockSpec(memory_space=pl.ANY)
-    gathered = pl.pallas_call(
+    packed = pltpu.VMEM((channels // 2, rows, 2 * lanes), jnp.bfloat16)
+    held = pltpu.VMEM((channels, tokens), jnp.bfloat16)
+    return pl.pallas_call(
         functools.partial(fused_kernel, ctx_count, chan_count),
-        in_specs=[VMEM] + [hbm] * 6,
+        in_specs=[pl.BlockSpec(memory_space=pltpu.SMEM)] + [hbm] * 9,
         out_specs=VMEM,
-        out_shape=jax.ShapeDtypeStruct((channels // 2, rows, 2 * lanes), jnp.bfloat16),
+        out_shape=jax.ShapeDtypeStruct((channels, tokens), jnp.bfloat16),
         scratch_shapes=[pltpu.VMEM(t.shape, t.dtype) for t in tables]
         + [
             pltpu.VMEM((2 * local_channels, block, lanes), jnp.float32),
@@ -346,16 +375,19 @@
             pltpu.VMEM((pairs, rows_total, 2 * lanes), jnp.bfloat16),
             pltpu.VMEM((pairs, rows_total, 2 * lanes), jnp.bfloat16),
             pltpu.VMEM((2 * rows_total, 2 * lanes), jnp.bfloat16),
+            held, held, held, packed, packed,
         ]
         + [sems(pairs, count - 1) for count in (total, total, ctx_count, ctx_count, total, total)]
-        + [sems(6)],
+        + [sems(9)],
         compiler_params=pltpu.CompilerParams(collective_id=0, has_side_effects=True),
-    )(paired, spectra.reshape(2 * local_channels, block, lanes), *tables)
-    tokens_conv = gathered.reshape(channels // 2, rows, 2, lanes).swapaxes(1, 2).reshape(channels, tokens)
-    result = gate_branch.astype(jnp.float32) * (
-        tokens_conv.astype(jnp.float32) + skip_gain[:, None] * carried.astype(jnp.float32)
-    )
-    return result.astype(jnp.bfloat16)
+    )(
+        skip_gain,
+        value_branch,
+        key_branch,
+        gate_branch,
+        spectra.reshape(2 * local_channels, block, lanes),
+        *tables,
+    )
 
 
 def body(value_branch, key_branch, gate_branch, skip_gain, spectra):
@@ -365,6 +397,7 @@
     block_rows = tokens * chan_count // lanes
     fits = (
         channels % (2 * total) == 0
+        and ctx_count % 8 == 0
         and tokens % (16 * lanes) == 0
         and block_rows <= lanes
         and lanes % block_rows == 0

time: 63 us -> 56.9 us (0.903)
  local copies, waits for them, and re-layouts: 5.76 us -> 2.09 us
  other arithmetic: 3.56 us -> 0 us
  Pallas kernels: 53.4 us -> 54.6 us
    convert_element_type x2 -> x0, local copies, waits for them, and re-layouts: 2.14 us -> none  [channel_body(): tokens_conv.astype(jnp.float32)]
    reshape x2 -> x0, local copies, waits for them, and re-layouts: 2 us -> none  [channel_body(): carried.reshape(channels // 2, 2, rows, lanes).swapaxes(1, 2)]
    convert_element_type x1 -> x0, other arithmetic: 1.95 us -> none  [channel_body(): return result.astype(jnp.bfloat16)]
    unnamed x1 -> x0, other arithmetic: 1.61 us -> none
    pallas_call x1, Pallas kernels: 53.4 us -> 54.6 us  [channel_body(): pl.pallas_call(functools.partial(fused_kernel, ctx_count, chan_count), in...]
    unnamed x9 -> x1, local copies, waits for them, and re-layouts: 1.61 us -> 2.09 us
where the time goes in v1:
time: 56.9 us; the launch traced here: 56.7 us
  Pallas kernels  54.6 us (96%)
  local copies, waits for them, and re-layouts  2.09 us (4%)
    pallas_call x1, Pallas kernels, channel_body(): pl.pallas_call(functools.partial(fused_kernel, ctx_count, chan_count), in...  54.6 us
    unnamed x1, local copies, waits for them, and re-layouts  2.09 us

profile of v1, /device:TPU:0, one launch (start us, length us, event | category | flops | bytes accessed | tf_op | source)
XLA Modules:
  0.0 56.7 jit_solution(11096040114054346276)
XLA Ops:
  0.0 54.6 %shard_map.100 = bf16[192,2048]{1,0:T(8,128)(2,1)} custom-call(f32[192]{0:T(256)} %skip_ref.1, bf16[192,2048]{1,0:T(8,128)(2,1)} %v_hbm.1, bf16[192,2048]{1,0:T(8,128)(2,1)} %k_hbm.1, bf16[192,2048]{1,0:T(8,128)(2,1)} %gate_hbm.1, f32[96,64,128]{2,1,0:T(8,128)} %bitcast.1, bf16[2,512,512]{2,1,0:T(8,128)(2,1)} %constant.10.clone.refs_0_, ...), custom_call_target="tpu_custom_call" | custom-call | tf_op jit(solution)/shard_map/pallas_call | solution.py:365
  54.7 2.1 %copy.12 = bf16[192,2048]{1,0:T(8,128)(2,1)} copy(bf16[192,2048]{1,0:T(8,128)(2,1)} %shard_map.100) | data formatting | bytes 1572864

commit v2 on v1

--- a/solution.py
+++ b/solution.py
@@ -203,15 +203,16 @@
     loads[0].wait()
     loads[1].wait()
 
-    @pl.loop(0, v_ref.shape[0] // group)
-    def _(index):
-        at = pl.ds(pl.multiple_of(index * group, group), group)
-        product = (k_ref[at].astype(jnp.float32) * v_ref[at].astype(jnp.float32)).astype(jnp.bfloat16)
-        split = product.astype(jnp.float32).reshape(ctx_count, 2, rows, lanes)
-        packed = jnp.concatenate([split[:, 0], split[:, 1]], axis=2)
-        c_ref[pl.ds(index * ctx_count, ctx_count)] = packed.astype(jnp.bfloat16)
-
-    pl.semaphore_wait(pltpu.get_barrier_semaphore(), total - 1)
+    def pack(pair):
+        @pl.loop(0, chan_count)
+        def _(chan_index):
+            index = chan_index * pairs + pair
+            at = pl.ds(pl.multiple_of(index * group, group), group)
+            product = (k_ref[at].astype(jnp.float32) * v_ref[at].astype(jnp.float32)).astype(jnp.bfloat16)
+            split = product.astype(jnp.float32).reshape(ctx_count, 2, rows, lanes)
+            packed = jnp.concatenate([split[:, 0], split[:, 1]], axis=2)
+            c_ref[pl.ds(index * ctx_count, ctx_count)] = packed.astype(jnp.bfloat16)
+
 
     def place(offset):
         other = lax.rem(me + offset, total)
@@ -266,12 +267,7 @@
         pieces = [flipped[f * block : (f + 1) * block] for f in range(flipped.shape[0] // block)]
         return jnp.concatenate(pieces, axis=1).astype(jnp.bfloat16)
 
-    start = lambda copy: copy.start()
-    for pair in range(pairs):
-        each(carried_copy, pair, total, start)
-        if pair == 0:
-            loads[2].wait()
-
+    def turn(pair):
         @pl.loop(1, ctx_count)
         def _(offset):
             first = (pair * ctx_count + lax.rem(ctx + offset, ctx_count)) * 2
@@ -283,8 +279,18 @@
             for which in range(2):
                 r_ref[part, 2 * pair + which, my_block] = turned(part, (pair * ctx_count + ctx) * 2 + which)
         x_ref[pair, my_rows] = c_ref[slot(ctx, chan, pair)]
+
+    start = lambda copy: copy.start()
+    pack(0)
+    pl.semaphore_wait(pltpu.get_barrier_semaphore(), total - 1)
+    each(carried_copy, 0, total, start)
+    for pair in range(1, pairs):
+        pack(pair)
+        each(carried_copy, pair, total, start)
+    loads[2].wait()
+    for pair in range(pairs):
+        turn(pair)
         each(spectra_copy, pair, ctx_count, start)
-
     for load in loads[3:]:
         load.wait()
     chunk = 2 * lanes

time: 56.9 us -> 56 us (0.984)
  Pallas kernels: 54.6 us -> 53.8 us
    pallas_call x1, Pallas kernels: 54.6 us -> 53.8 us  [channel_body(): pl.pallas_call(functools.partial(fused_kernel, ctx_count, chan_count), in...]
where the time goes in v2:
time: 56 us; the launch traced here: 55.9 us
  Pallas kernels  53.8 us (96%)
  local copies, waits for them, and re-layouts  2.09 us (4%)
    pallas_call x1, Pallas kernels, channel_body(): pl.pallas_call(functools.partial(fused_kernel, ctx_count, chan_count), in...  53.8 us
    unnamed x1, local copies, waits for them, and re-layouts  2.09 us

profile of v2, /device:TPU:0, one launch (start us, length us, event | category | flops | bytes accessed | tf_op | source)
XLA Modules:
  0.0 55.9 jit_solution(17769067251820746361)
XLA Ops:
  0.0 53.8 %shard_map.100 = bf16[192,2048]{1,0:T(8,128)(2,1)} custom-call(f32[192]{0:T(256)} %skip_ref.1, bf16[192,2048]{1,0:T(8,128)(2,1)} %v_hbm.1, bf16[192,2048]{1,0:T(8,128)(2,1)} %k_hbm.1, bf16[192,2048]{1,0:T(8,128)(2,1)} %gate_hbm.1, f32[96,64,128]{2,1,0:T(8,128)} %bitcast.1, bf16[2,512,512]{2,1,0:T(8,128)(2,1)} %constant.10.clone.refs_0_, ...), custom_call_target="tpu_custom_call" | custom-call | tf_op jit(solution)/shard_map/pallas_call | solution.py:371
  53.8 2.1 %copy.12 = bf16[192,2048]{1,0:T(8,128)(2,1)} copy(bf16[192,2048]{1,0:T(8,128)(2,1)} %shard_map.100) | data formatting | bytes 1572864
